TPU v7x, 128 devices: a whole 4x4x4 slice. The times are simulated.
128 devices in a mesh: feat: 64 (over x, y, z_lo, core), rows: 2 (over z_hi).
Axes of the slice: x: 4, y: 4, z: 4 (z_hi: 2, z_lo: 2; z = z_hi * 2 + z_lo), core: 2. Of those that a mesh axis runs over, the one named last changes fastest.
Arguments:
- embeddings: bfloat16 [256, 512], P('rows'), may hold values from -6 to 6
- sign_flips: float32 [524288], P('feat'), may hold values from -1 to 1, as said below
- gaussian: float32 [524288], P('feat'), may hold values from -5 to 5
- scales: float32 [524288], P('feat'), may hold values from 0.5 to 2
- phases: float32 [524288], P('feat'), may hold values from 0 to 6.2831855
- source_blocks: int32 [4096], P('feat'), may hold values from 0 to 4095, as said below
- block_permutations: bfloat16 [4096, 128, 128], P('feat'), may hold values from 0 to 1, as said below
- weights: float32 [524288], P('feat'), may hold values from -6 to 6
- targets: float32 [256], P('rows'), may hold values from -6 to 6
Outputs:
- predictions: float32 [256], P('rows')
- feature_grad: float32 [524288], P(('feat', 'rows'))
Inputs may be any that keep to these rules, and one draw needn't show every extreme that they name: `sign_flips`: each entry is -1 or 1. `source_blocks`: A permutation of the 4096 block numbers. The 64 entries of each aligned run of 64 entries name exactly 1 block from every aligned run of 64 blocks. Each block_permutations[b] is a permutation matrix.
All inputs are finite; a program needn't handle non-finite values.
Results may differ from a plain program's by a relative error of at most 0.0003.
Values sent between devices are 32-bit elements; how exact they have to be, the bound alone decides.
A program may use at most 64 MiB of HBM per device.

v0:
```python
import math
import jax
import jax.numpy as jnp
from jax import lax
from jax.sharding import PartitionSpec as P

FEATURE_COUNT = 524288


def rademacher_signs(length):
    indices = jnp.arange(length, dtype=jnp.int32)
    joined = jnp.bitwise_and(indices[:, None], indices[None, :])
    parity = jnp.zeros((length, length), jnp.int32)
    for bit_number in range(length.bit_length() - 1):
        parity = parity + jnp.bitwise_and(jnp.right_shift(joined, bit_number), 1)
    return (1 - 2 * jnp.bitwise_and(parity, 1)).astype(jnp.float32)


def transform(field, block):
    row_count = field.shape[0]
    feat_here = field.shape[1]
    outer = feat_here // block
    values = field.reshape(row_count, outer, block)
    values = jnp.einsum(
        "rac,dc->rad", values, rademacher_signs(block), precision=lax.Precision.HIGHEST
    )
    values = jnp.einsum(
        "rac,ba->rbc", values, rademacher_signs(outer), precision=lax.Precision.HIGHEST
    )
    device_shards = lax.axis_size("feat")
    spread = values
    across_devices = lax.all_to_all(spread, "feat", split_axis=1, concat_axis=1, tiled=True)
    combined = jnp.einsum(
        "gwf,aw->gaf",
        across_devices,
        rademacher_signs(device_shards),
        precision=lax.Precision.HIGHEST,
    )
    returned = lax.all_to_all(combined, "feat", split_axis=1, concat_axis=1, tiled=True)
    values = returned.reshape(row_count, feat_here)
    return values * (1.0 / math.sqrt(FEATURE_COUNT))


def local(
    embeddings,
    sign_flips,
    gaussian,
    scales,
    phases,
    source_blocks,
    block_permutations,
    weights,
    targets,
):
    row_count = embeddings.shape[0]
    width = embeddings.shape[1]
    feat_here = sign_flips.shape[0]
    blk_here = block_permutations.shape[0]
    block = block_permutations.shape[1]
    device_shards = lax.axis_size("feat")
    per_pair = blk_here // device_shards
    tiled = jnp.tile(embeddings.astype(jnp.float32), (1, feat_here // width)) * sign_flips[None, :]
    first = transform(tiled, block)
    source_dev = source_blocks // blk_here
    source_local = source_blocks % blk_here
    slot_keys = source_dev * blk_here + jnp.arange(blk_here, dtype=jnp.int32)
    ordering = jnp.argsort(slot_keys)
    inverse = jnp.argsort(ordering)
    wanted = jnp.take(source_local, ordering).reshape(device_shards, per_pair)
    asked = lax.all_to_all(wanted, "feat", split_axis=0, concat_axis=0, tiled=True)
    first_blocks = first.reshape(row_count, blk_here, block)
    outgoing = jnp.take(first_blocks, asked.reshape(-1), axis=1)
    incoming = lax.all_to_all(outgoing, "feat", split_axis=1, concat_axis=1, tiled=True)
    placed = jnp.take(incoming, inverse, axis=1)
    mixed = jnp.einsum(
        "rbj,bij->rbi",
        placed,
        block_permutations.astype(jnp.float32),
        precision=lax.Precision.HIGHEST,
    )
    mixed = mixed.reshape(row_count, feat_here) * gaussian[None, :]
    second = transform(mixed, block)
    features = jnp.cos(scales[None, :] * second + phases[None, :])
    local_sum = jnp.dot(features, weights, precision=lax.Precision.HIGHEST)
    predictions = lax.psum(local_sum, "feat") * (1.0 / math.sqrt(FEATURE_COUNT))
    residual = predictions - targets
    total_rows = row_count * lax.axis_size("rows")
    grad_terms = jnp.dot(residual, features, precision=lax.Precision.HIGHEST) * (
        1.0 / math.sqrt(total_rows)
    )
    feature_grad = lax.psum_scatter(grad_terms, "rows", scatter_dimension=0, tiled=True)
    return (predictions, feature_grad)


def solution(mesh):
    in_specs = (
        P("rows", None),
        P("feat"),
        P("feat"),
        P("feat"),
        P("feat"),
        P("feat"),
        P("feat", None, None),
        P("feat"),
        P("rows"),
    )
    out_specs = (P("rows"), P(("feat", "rows")))
    return jax.shard_map(local, mesh=mesh, in_specs=in_specs, out_specs=out_specs, check_vma=False)
```

profile of v0, /device:TPU:0, one launch (start us, length us, event | category | flops | bytes accessed | tf_op | source)
XLA Modules:
  0.0 581.3 jit_solution(2201603233594802488)
XLA Ops:
  0.6 3.5 tile.4
  4.2 4.8 tile.10
  8.9 6.5 %fusion.11 = f32[128,64,128]{2,1,0:T(8,128)S(1)} fusion(f32[128,64,128]{2,1,0:T(8,128)} %tile.10, f32[64,128]{1,0:T(8,128)S(1)} %bitcast.56), kind=kOutput, calls=%fused_computation.17 | convolution fusion | flops 1612070912 | bytes 8421376 | tf_op jit(solution)/shard_map/rac,dc->rad/dot_general | solution.py:24
  15.5 3.9 convolution_bitcast_fusion.1
  19.3 4.4 copy.25
  23.7 9.8 %all-to-all-start = ((f32[128,64,128]{2,0,1:T(8,128)}), f32[128,64,128]{2,0,1:T(8,128)}, u32[]{:S(2)}, u32[]{:S(2)}) async-start(f32[128,64,128]{2,0,1:T(8,128)} %copy.25), calls=%async_computation | async-start | bytes 8388608 | tf_op jit(solution)/shard_map/all_to_all | solution.py:32
  37.1 47.5 %all-to-all-done = f32[128,64,128]{2,0,1:T(8,128)} async-done(((f32[128,64,128]{2,0,1:T(8,128)}), f32[128,64,128]{2,0,1:T(8,128)}, u32[]{:S(2)}, u32[]{:S(2)}) %all-to-all-start) | async-done | bytes 4194336 | tf_op jit(solution)/shard_map/all_to_all | solution.py:32
  84.6 9.3 %all-to-all-start.2 = ((s32[64,1,1]{2,1,0:T(1,128)}), s32[64,1,1]{2,1,0:T(1,128)S(1)}, u32[]{:S(2)}, u32[]{:S(2)}) async-start(s32[64,1,1]{2,1,0:T(1,128)} %copy.24), calls=%async_computation.2 | async-start | bytes 65536 | tf_op jit(solution)/shard_map/all_to_all | solution.py:70
  93.9 8.4 %fusion.13 = f32[128,64,128]{2,1,0:T(8,128)S(1)} fusion(f32[128,64,128]{2,0,1:T(8,128)} %all-to-all-done), kind=kOutput, calls=%fused_computation.19 | convolution fusion | flops 805396480 | bytes 8388608 | tf_op jit(solution)/shard_map/gwf,aw->gaf/dot_general | solution.py:33
  102.3 4.4 copy.27
  106.7 9.2 %all-to-all-start.1 = ((f32[128,64,128]{2,0,1:T(8,128)}), f32[128,64,128]{2,0,1:T(8,128)}, u32[]{:S(2)}, u32[]{:S(2)}) async-start(f32[128,64,128]{2,0,1:T(8,128)} %copy.27), calls=%async_computation.1 | async-start | bytes 8388608 | tf_op jit(solution)/shard_map/all_to_all | solution.py:39
  117.2 49.8 %all-to-all-done.1 = f32[128,64,128]{2,0,1:T(8,128)} async-done(((f32[128,64,128]{2,0,1:T(8,128)}), f32[128,64,128]{2,0,1:T(8,128)}, u32[]{:S(2)}, u32[]{:S(2)}) %all-to-all-start.1) | async-done | bytes 4194336 | tf_op jit(solution)/shard_map/all_to_all | solution.py:39
  167.1 4.9 broadcast_multiply_fusion
  172.0 4.9 gather_fusion.1
  176.9 4.5 select_bitcast_fusion
  181.3 9.4 %all-to-all-start.3 = ((f32[128,64,128]{2,0,1:T(8,128)}), f32[128,64,128]{2,0,1:T(8,128)}, u32[]{:S(2)}, u32[]{:S(2)}) async-start(f32[128,64,128]{2,0,1:T(8,128)} %select_bitcast_fusion), calls=%async_computation.3 | async-start | bytes 8388608 | tf_op jit(solution)/shard_map/all_to_all | solution.py:73
  192.8 49.0 %all-to-all-done.3 = f32[128,64,128]{2,0,1:T(8,128)} async-done(((f32[128,64,128]{2,0,1:T(8,128)}), f32[128,64,128]{2,0,1:T(8,128)}, u32[]{:S(2)}, u32[]{:S(2)}) %all-to-all-start.3) | async-done | bytes 4194336 | tf_op jit(solution)/shard_map/all_to_all | solution.py:73
  241.8 4.9 gather_fusion.2
  246.7 6.5 %multiply_bitcast_fusion = f32[128,64,128]{2,0,1:T(8,128)S(1)} fusion(bf16[64,128,128]{2,1,0:T(8,128)(2,1)S(1)} %copy-done, f32[64,128,128]{2,1,0:T(8,128)} %gather_fusion.2, f32[64,128]{1,0:T(8,128)S(1)} %bitcast.57, pred[64]{0:T(512)(128)(4,1)S(1)} %compare_and_fusion), kind=kOutput, calls=%fused_computation.16 | convolution fusion | flops 1612709888 | bytes 10518592 | tf_op jit(solution)/shard_map/rbj,bij->rbi/dot_general | solution.py:75
  253.3 6.5 %fusion.6 = f32[128,64,128]{2,1,0:T(8,128)S(1)} fusion(f32[128,64,128]{2,0,1:T(8,128)S(1)} %multiply_bitcast_fusion), kind=kOutput, calls=%fused_computation.10 | convolution fusion | flops 1611022336 | bytes 8388608 | tf_op jit(solution)/shard_map/rac,dc->rad/dot_general | solution.py:24
  259.8 3.9 convolution_bitcast_fusion
  263.7 2.8 copy.29
  266.5 60.0 %all_to_all.31 = f32[128,64,128]{2,0,1:T(8,128)S(1)} all-to-all(f32[128,64,128]{2,0,1:T(8,128)S(1)} %copy.29), channel_id=1, replica_groups=mesh['feat'=64,'rows'=2] {'feat'}, dimensions={1} | all-to-all | bytes 8388608 | tf_op jit(solution)/shard_map/all_to_all | solution.py:32
  326.5 6.0 %fusion.16 = f32[128,64,128]{2,1,0:T(8,128)S(1)} fusion(f32[128,64,128]{2,0,1:T(8,128)S(1)} %all_to_all.31), kind=kOutput, calls=%fused_computation.20 | convolution fusion | flops 805396480 | bytes 8388608 | tf_op jit(solution)/shard_map/gwf,aw->gaf/dot_general | solution.py:33
  332.5 4.4 copy.31
  336.9 6.1 %all-to-all-start.5 = ((f32[128,64,128]{2,0,1:T(8,128)}), f32[128,64,128]{2,0,1:T(8,128)}, u32[]{:S(2)}, u32[]{:S(2)}) async-start(f32[128,64,128]{2,0,1:T(8,128)} %copy.31), calls=%async_computation.5 | async-start | bytes 8388608 | tf_op jit(solution)/shard_map/all_to_all | solution.py:39
  344.3 49.6 %all-to-all-done.5 = f32[128,64,128]{2,0,1:T(8,128)} async-done(((f32[128,64,128]{2,0,1:T(8,128)}), f32[128,64,128]{2,0,1:T(8,128)}, u32[]{:S(2)}, u32[]{:S(2)}) %all-to-all-start.5) | async-done | bytes 4194336 | tf_op jit(solution)/shard_map/all_to_all | solution.py:39
  393.9 5.6 copy.32
  399.5 16.6 %fusion.1 = f32[128,8192]{0,1:T(8,128)S(1)} fusion(f32[128,64,128]{0,2,1:T(8,128)} %copy.32, f32[8192]{0:T(1024)S(1)} %copy-done.5, f32[8192]{0:T(1024)S(1)} %broadcast_multiply_fusion.2), kind=kLoop, calls=%fused_computation.5 | loop fusion | flops 2097152 | bytes 8454144 | tf_op jit(solution)/shard_map/cos | solution.py:83
  420.6 142.3 %psum.7 = f32[128]{0:T(128)S(1)} all-reduce(f32[128]{0:T(128)S(1)} %convolution_bitcast_fusion.2), channel_id=1, replica_groups=mesh['feat'=64,'rows'=2] {'feat'}, use_global_device_ids=true, to_apply=%region_2.4 | all-reduce | flops 128 | bytes 1024 | tf_op jit(solution)/shard_map/psum | solution.py:85
  562.9 5.6 fusion.36
  568.6 11.9 %all-reduce = f32[8192]{0:T(1024)S(1)} all-reduce(f32[8192]{0:T(1024)S(1)} %broadcast_multiply_fusion.1), channel_id=2, replica_groups=mesh['feat'=64,'rows'=2] {'rows'}, use_global_device_ids=true, to_apply=%region_3.5.clone | all-reduce | flops 8192 | bytes 65536
  (48 shorter events, 12.6 us)
Async XLA Ops:
  0.6 246.1 %copy-start = (bf16[64,128,128]{2,1,0:T(8,128)(2,1)S(1)}, bf16[64,128,128]{2,1,0:T(8,128)(2,1)}, u32[]{:S(2)}) copy-start(bf16[64,128,128]{2,1,0:T(8,128)(2,1)} %param.17) | copy-start | bytes 6291460
  4.2 4.8 copy-start.3
  23.7 9.8 %copy-start.10 = (s32[64]{0:T(128)S(1)}, s32[64]{0:T(128)}, u32[]{:S(2)}) copy-start(s32[64]{0:T(128)} %param.16) | copy-start | bytes 772
  23.7 60.9 %all-to-all-start = ((f32[128,64,128]{2,0,1:T(8,128)}), f32[128,64,128]{2,0,1:T(8,128)}, u32[]{:S(2)}, u32[]{:S(2)}) async-start(f32[128,64,128]{2,0,1:T(8,128)} %copy.25), calls=%async_computation | async-start | bytes 8388608 | tf_op jit(solution)/shard_map/all_to_all | solution.py:32
  84.6 22.1 %all-to-all-start.2 = ((s32[64,1,1]{2,1,0:T(1,128)}), s32[64,1,1]{2,1,0:T(1,128)S(1)}, u32[]{:S(2)}, u32[]{:S(2)}) async-start(s32[64,1,1]{2,1,0:T(1,128)} %copy.24), calls=%async_computation.2 | async-start | bytes 65536 | tf_op jit(solution)/shard_map/all_to_all | solution.py:70
  106.7 60.3 %all-to-all-start.1 = ((f32[128,64,128]{2,0,1:T(8,128)}), f32[128,64,128]{2,0,1:T(8,128)}, u32[]{:S(2)}, u32[]{:S(2)}) async-start(f32[128,64,128]{2,0,1:T(8,128)} %copy.27), calls=%async_computation.1 | async-start | bytes 8388608 | tf_op jit(solution)/shard_map/all_to_all | solution.py:39
  181.3 60.5 %all-to-all-start.3 = ((f32[128,64,128]{2,0,1:T(8,128)}), f32[128,64,128]{2,0,1:T(8,128)}, u32[]{:S(2)}, u32[]{:S(2)}) async-start(f32[128,64,128]{2,0,1:T(8,128)} %select_bitcast_fusion), calls=%async_computation.3 | async-start | bytes 8388608 | tf_op jit(solution)/shard_map/all_to_all | solution.py:73
  192.8 54.0 %copy-start.4 = (f32[8192]{0:T(1024)S(1)}, f32[8192]{0:T(1024)}, u32[]{:S(2)}) copy-start(f32[8192]{0:T(1024)} %param.13) | copy-start | bytes 98308
  336.9 6.1 %copy-start.11 = (u32[128]{0:T(128)S(1)}, u32[128]{0:T(128)}, u32[]{:S(2)}) copy-start(u32[128]{0:T(128)} %constant.76) | copy-start | bytes 1540
  336.9 7.4 %copy-start.7 = (f32[8192]{0:T(1024)S(1)}, f32[8192]{0:T(1024)}, u32[]{:S(2)}) copy-start(f32[8192]{0:T(1024)} %param.14) | copy-start | bytes 98308
  336.9 57.0 %all-to-all-start.5 = ((f32[128,64,128]{2,0,1:T(8,128)}), f32[128,64,128]{2,0,1:T(8,128)}, u32[]{:S(2)}, u32[]{:S(2)}) async-start(f32[128,64,128]{2,0,1:T(8,128)} %copy.31), calls=%async_computation.5 | async-start | bytes 8388608 | tf_op jit(solution)/shard_map/all_to_all | solution.py:39
  344.3 55.2 %copy-start.5 = (f32[8192]{0:T(1024)S(1)}, f32[8192]{0:T(1024)}, u32[]{:S(2)}) copy-start(f32[8192]{0:T(1024)} %param.15) | copy-start | bytes 98308
  399.5 18.8 %copy-start.6 = (f32[8192]{0:T(1024)S(1)}, f32[8192]{0:T(1024)}, u32[]{:S(2)}) copy-start(f32[8192]{0:T(1024)} %param.18) | copy-start | bytes 98308
  416.1 2.1 copy-start.2
  416.1 146.8 %copy-start.8 = (f32[128]{0:T(128)S(1)}, f32[128]{0:T(128)}, u32[]{:S(2)}) copy-start(f32[128]{0:T(128)} %param.19) | copy-start | bytes 1540
  416.1 165.0 %copy-start.1 = (bf16[64,128,128]{2,1,0:T(8,128)(2,1)S(1)}, bf16[64,128,128]{2,1,0:T(8,128)(2,1)}, u32[]{:S(2)}) copy-start(bf16[64,128,128]{2,1,0:T(8,128)(2,1)} %param.17) | copy-start | bytes 6291460
  562.9 18.2 %copy-start.9 = (f32[128]{0:T(128)}, f32[128]{0:T(128)S(1)}, u32[]{:S(2)}) copy-start(f32[128]{0:T(128)S(1)} %broadcast_multiply_fusion.3) | copy-start | bytes 1540
where the time goes:
time: 591 us; the launch traced here: 581 us
  blocking collectives  214 us (36%)
  waiting for transfers between devices  196 us (33%)
  matrix products  49.6 us (8%)
  local copies, waits for them, and re-layouts  44.6 us (8%)
  starting transfers between devices  43.8 us (7%)
  other arithmetic  31.4 us (5%)
    psum x1, blocking collectives, local(): predictions = lax.psum(local_sum, 'feat') * (1.0 / math.sqrt(FEATURE_COUNT))  142 us
    all_to_all x2, waiting for transfers between devices, transform(): lax.all_to_all(combined, 'feat', split_axis=1, concat_axis=1, tiled=True)  99.5 us
    all_to_all x1, blocking collectives, transform(): lax.all_to_all(spread, 'feat', split_axis=1, concat_axis=1, tiled=True)  60 us
    all_to_all x1, waiting for transfers between devices, local(): lax.all_to_all(outgoing, 'feat', split_axis=1, concat_axis=1, tiled=True)  49 us
    all_to_all x1, waiting for transfers between devices, transform(): lax.all_to_all(spread, 'feat', split_axis=1, concat_axis=1, tiled=True)  47.5 us
    cos x1, other arithmetic, local(): features = jnp.cos(scales[None, :] * second + phases[None, :])  16.6 us
    all_to_all x2, starting transfers between devices, transform(): lax.all_to_all(combined, 'feat', split_axis=1, concat_axis=1, tiled=True)  15.3 us
    dot_general x2, matrix products, transform(): jnp.einsum('gwf,aw->gaf', across_devices, rademacher_signs(device_shards)...  14.4 us
  transfers between devices with their start and end apart: 5, of which 4 were waited for; matrix products, arithmetic and copies ran while one was open for 3% of the time, Pallas kernels for 0%

commit v1 on v0

--- a/solution.py
+++ b/solution.py
@@ -3,6 +3,7 @@
 import jax.numpy as jnp
 from jax import lax
 from jax.sharding import PartitionSpec as P
+from jax.lax import all_gather
 
 FEATURE_COUNT = 524288
 
@@ -82,7 +83,7 @@
     second = transform(mixed, block)
     features = jnp.cos(scales[None, :] * second + phases[None, :])
     local_sum = jnp.dot(features, weights, precision=lax.Precision.HIGHEST)
-    predictions = lax.psum(local_sum, "feat") * (1.0 / math.sqrt(FEATURE_COUNT))
+    predictions = jnp.sum(all_gather(local_sum, "feat"), 0) * (1.0 / math.sqrt(FEATURE_COUNT))
     residual = predictions - targets
     total_rows = row_count * lax.axis_size("rows")
     grad_terms = jnp.dot(residual, features, precision=lax.Precision.HIGHEST) * (

time: 591 us -> 529 us (0.90)
  blocking collectives: 214 us -> 152 us
    psum x1 -> x0, blocking collectives: 142 us -> none  [local(): predictions = lax.psum(local_sum, 'feat') * (1.0 / math.sqrt(FEATURE_COUNT))]
    all_gather x0 -> x1, blocking collectives: none -> 80.4 us  [local(): all_gather(local_sum, 'feat')]
  transfers between devices with their start and end apart: 5 -> 5, of which waited for: 4 -> 4; matrix products, arithmetic and copies ran while one was open for 3% -> 4% of each run, Pallas kernels for 0% -> 0%
where the time goes in v1:
time: 529 us; the launch traced here: 520 us
  waiting for transfers between devices  196 us (37%)
  blocking collectives  152 us (29%)
  matrix products  49.6 us (9%)
  local copies, waits for them, and re-layouts  44.6 us (8%)
  starting transfers between devices  43.8 us (8%)
  other arithmetic  31.5 us (6%)
    all_to_all x2, waiting for transfers between devices, transform(): lax.all_to_all(combined, 'feat', split_axis=1, concat_axis=1, tiled=True)  99.5 us
    all_gather x1, blocking collectives, local(): all_gather(local_sum, 'feat')  80.4 us
    all_to_all x1, blocking collectives, transform(): lax.all_to_all(spread, 'feat', split_axis=1, concat_axis=1, tiled=True)  60 us
    all_to_all x1, waiting for transfers between devices, local(): lax.all_to_all(outgoing, 'feat', split_axis=1, concat_axis=1, tiled=True)  49 us
    all_to_all x1, waiting for transfers between devices, transform(): lax.all_to_all(spread, 'feat', split_axis=1, concat_axis=1, tiled=True)  47.5 us
    cos x1, other arithmetic, local(): features = jnp.cos(scales[None, :] * second + phases[None, :])  16.6 us
    all_to_all x2, starting transfers between devices, transform(): lax.all_to_all(combined, 'feat', split_axis=1, concat_axis=1, tiled=True)  15.3 us
    dot_general x2, matrix products, transform(): jnp.einsum('gwf,aw->gaf', across_devices, rademacher_signs(device_shards)...  14.4 us
  transfers between devices with their start and end apart: 5, of which 4 were waited for; matrix products, arithmetic and copies ran while one was open for 4% of the time, Pallas kernels for 0%

profile of v1, /device:TPU:0, one launch (start us, length us, event | category | flops | bytes accessed | tf_op | source)
XLA Modules:
  0.0 519.5 jit_solution(9048397947707734252)
XLA Ops:
  0.6 3.5 tile.4
  4.2 4.8 tile.10
  8.9 6.5 %fusion.11 = f32[128,64,128]{2,1,0:T(8,128)S(1)} fusion(f32[128,64,128]{2,1,0:T(8,128)} %tile.10, f32[64,128]{1,0:T(8,128)S(1)} %bitcast.58), kind=kOutput, calls=%fused_computation.17 | convolution fusion | flops 1612070912 | bytes 8421376 | tf_op jit(solution)/shard_map/rac,dc->rad/dot_general | solution.py:25
  15.5 3.9 convolution_bitcast_fusion.1
  19.3 4.4 copy.25
  23.7 9.8 %all-to-all-start = ((f32[128,64,128]{2,0,1:T(8,128)}), f32[128,64,128]{2,0,1:T(8,128)}, u32[]{:S(2)}, u32[]{:S(2)}) async-start(f32[128,64,128]{2,0,1:T(8,128)} %copy.25), calls=%async_computation | async-start | bytes 8388608 | tf_op jit(solution)/shard_map/all_to_all | solution.py:33
  37.1 47.5 %all-to-all-done = f32[128,64,128]{2,0,1:T(8,128)} async-done(((f32[128,64,128]{2,0,1:T(8,128)}), f32[128,64,128]{2,0,1:T(8,128)}, u32[]{:S(2)}, u32[]{:S(2)}) %all-to-all-start) | async-done | bytes 4194336 | tf_op jit(solution)/shard_map/all_to_all | solution.py:33
  84.6 9.3 %all-to-all-start.2 = ((s32[64,1,1]{2,1,0:T(1,128)}), s32[64,1,1]{2,1,0:T(1,128)S(1)}, u32[]{:S(2)}, u32[]{:S(2)}) async-start(s32[64,1,1]{2,1,0:T(1,128)} %copy.24), calls=%async_computation.2 | async-start | bytes 65536 | tf_op jit(solution)/shard_map/all_to_all | solution.py:71
  93.9 8.4 %fusion.13 = f32[128,64,128]{2,1,0:T(8,128)S(1)} fusion(f32[128,64,128]{2,0,1:T(8,128)} %all-to-all-done), kind=kOutput, calls=%fused_computation.19 | convolution fusion | flops 805396480 | bytes 8388608 | tf_op jit(solution)/shard_map/gwf,aw->gaf/dot_general | solution.py:34
  102.3 4.4 copy.27
  106.7 9.2 %all-to-all-start.1 = ((f32[128,64,128]{2,0,1:T(8,128)}), f32[128,64,128]{2,0,1:T(8,128)}, u32[]{:S(2)}, u32[]{:S(2)}) async-start(f32[128,64,128]{2,0,1:T(8,128)} %copy.27), calls=%async_computation.1 | async-start | bytes 8388608 | tf_op jit(solution)/shard_map/all_to_all | solution.py:40
  117.2 49.8 %all-to-all-done.1 = f32[128,64,128]{2,0,1:T(8,128)} async-done(((f32[128,64,128]{2,0,1:T(8,128)}), f32[128,64,128]{2,0,1:T(8,128)}, u32[]{:S(2)}, u32[]{:S(2)}) %all-to-all-start.1) | async-done | bytes 4194336 | tf_op jit(solution)/shard_map/all_to_all | solution.py:40
  167.1 4.9 broadcast_multiply_fusion
  172.0 4.9 gather_fusion.1
  176.9 4.5 select_bitcast_fusion
  181.3 9.4 %all-to-all-start.3 = ((f32[128,64,128]{2,0,1:T(8,128)}), f32[128,64,128]{2,0,1:T(8,128)}, u32[]{:S(2)}, u32[]{:S(2)}) async-start(f32[128,64,128]{2,0,1:T(8,128)} %select_bitcast_fusion), calls=%async_computation.3 | async-start | bytes 8388608 | tf_op jit(solution)/shard_map/all_to_all | solution.py:74
  192.8 49.0 %all-to-all-done.3 = f32[128,64,128]{2,0,1:T(8,128)} async-done(((f32[128,64,128]{2,0,1:T(8,128)}), f32[128,64,128]{2,0,1:T(8,128)}, u32[]{:S(2)}, u32[]{:S(2)}) %all-to-all-start.3) | async-done | bytes 4194336 | tf_op jit(solution)/shard_map/all_to_all | solution.py:74
  241.8 4.9 gather_fusion.2
  246.7 6.5 %multiply_bitcast_fusion = f32[128,64,128]{2,0,1:T(8,128)S(1)} fusion(bf16[64,128,128]{2,1,0:T(8,128)(2,1)S(1)} %copy-done, f32[64,128,128]{2,1,0:T(8,128)} %gather_fusion.2, f32[64,128]{1,0:T(8,128)S(1)} %bitcast.59, pred[64]{0:T(512)(128)(4,1)S(1)} %compare_and_fusion), kind=kOutput, calls=%fused_computation.16 | convolution fusion | flops 1612709888 | bytes 10518592 | tf_op jit(solution)/shard_map/rbj,bij->rbi/dot_general | solution.py:76
  253.3 6.5 %fusion.6 = f32[128,64,128]{2,1,0:T(8,128)S(1)} fusion(f32[128,64,128]{2,0,1:T(8,128)S(1)} %multiply_bitcast_fusion), kind=kOutput, calls=%fused_computation.10 | convolution fusion | flops 1611022336 | bytes 8388608 | tf_op jit(solution)/shard_map/rac,dc->rad/dot_general | solution.py:25
  259.8 3.9 convolution_bitcast_fusion
  263.7 2.8 copy.29
  266.5 60.0 %all_to_all.31 = f32[128,64,128]{2,0,1:T(8,128)S(1)} all-to-all(f32[128,64,128]{2,0,1:T(8,128)S(1)} %copy.29), channel_id=1, replica_groups=mesh['feat'=64,'rows'=2] {'feat'}, dimensions={1} | all-to-all | bytes 8388608 | tf_op jit(solution)/shard_map/all_to_all | solution.py:33
  326.5 6.0 %fusion.16 = f32[128,64,128]{2,1,0:T(8,128)S(1)} fusion(f32[128,64,128]{2,0,1:T(8,128)S(1)} %all_to_all.31), kind=kOutput, calls=%fused_computation.20 | convolution fusion | flops 805396480 | bytes 8388608 | tf_op jit(solution)/shard_map/gwf,aw->gaf/dot_general | solution.py:34
  332.5 4.4 copy.31
  336.9 6.1 %all-to-all-start.5 = ((f32[128,64,128]{2,0,1:T(8,128)}), f32[128,64,128]{2,0,1:T(8,128)}, u32[]{:S(2)}, u32[]{:S(2)}) async-start(f32[128,64,128]{2,0,1:T(8,128)} %copy.31), calls=%async_computation.5 | async-start | bytes 8388608 | tf_op jit(solution)/shard_map/all_to_all | solution.py:40
  344.3 49.6 %all-to-all-done.5 = f32[128,64,128]{2,0,1:T(8,128)} async-done(((f32[128,64,128]{2,0,1:T(8,128)}), f32[128,64,128]{2,0,1:T(8,128)}, u32[]{:S(2)}, u32[]{:S(2)}) %all-to-all-start.5) | async-done | bytes 4194336 | tf_op jit(solution)/shard_map/all_to_all | solution.py:40
  393.9 5.6 %copy.32 = f32[128,64,128]{0,2,1:T(8,128)} copy(f32[128,64,128]{2,0,1:T(8,128)} %all-to-all-done.5) | data formatting | bytes 8388608 | tf_op jit(solution)/shard_map/all_to_all | solution.py:40
  399.5 16.6 %fusion.1 = f32[128,8192]{0,1:T(8,128)S(1)} fusion(f32[128,64,128]{0,2,1:T(8,128)} %copy.32, f32[8192]{0:T(1024)S(1)} %copy-done.5, f32[8192]{0:T(1024)S(1)} %broadcast_multiply_fusion.2), kind=kLoop, calls=%fused_computation.5 | loop fusion | flops 2097152 | bytes 8454144 | tf_op jit(solution)/shard_map/cos | solution.py:84
  420.6 80.4 %all-gather.1 = f32[64,1,128]{2,1,0:T(1,128)S(1)} all-gather(f32[1,1,128]{2,1,0:T(1,128)S(1)} %convolution_bitcast_fusion.2), channel_id=2, replica_groups=mesh['feat'=64,'rows'=2] {'feat'}, dimensions={0}, use_global_device_ids=true | all-gather | bytes 33280 | tf_op jit(solution)/shard_map/all_gather | solution.py:86
  501.1 5.6 %fusion.36 = f32[1,8192]{1,0:T(1,128)S(1)} fusion(f32[128,8192]{0,1:T(8,128)} %copy-done.2, f32[128]{0:T(128)S(1)} %broadcast_multiply_fusion.3, f32[128]{0:T(128)S(1)} %copy-done.8), kind=kOutput, calls=%fused_computation.58 | convolution fusion | flops 12583040 | bytes 4228096 | tf_op jit(solution)/shard_map/dot_general | solution.py:89
  506.8 11.9 %all-reduce = f32[8192]{0:T(1024)S(1)} all-reduce(f32[8192]{0:T(1024)S(1)} %broadcast_multiply_fusion.1), channel_id=3, replica_groups=mesh['feat'=64,'rows'=2] {'rows'}, use_global_device_ids=true, to_apply=%region_3.5.clone | all-reduce | flops 8192 | bytes 65536
  (49 shorter events, 12.7 us)
Async XLA Ops:
  0.6 246.1 %copy-start = (bf16[64,128,128]{2,1,0:T(8,128)(2,1)S(1)}, bf16[64,128,128]{2,1,0:T(8,128)(2,1)}, u32[]{:S(2)}) copy-start(bf16[64,128,128]{2,1,0:T(8,128)(2,1)} %param.17) | copy-start | bytes 6291460
  4.2 4.8 copy-start.3
  23.7 9.8 %copy-start.10 = (s32[64]{0:T(128)S(1)}, s32[64]{0:T(128)}, u32[]{:S(2)}) copy-start(s32[64]{0:T(128)} %param.16) | copy-start | bytes 772
  23.7 60.9 %all-to-all-start = ((f32[128,64,128]{2,0,1:T(8,128)}), f32[128,64,128]{2,0,1:T(8,128)}, u32[]{:S(2)}, u32[]{:S(2)}) async-start(f32[128,64,128]{2,0,1:T(8,128)} %copy.25), calls=%async_computation | async-start | bytes 8388608 | tf_op jit(solution)/shard_map/all_to_all | solution.py:33
  84.6 22.1 %all-to-all-start.2 = ((s32[64,1,1]{2,1,0:T(1,128)}), s32[64,1,1]{2,1,0:T(1,128)S(1)}, u32[]{:S(2)}, u32[]{:S(2)}) async-start(s32[64,1,1]{2,1,0:T(1,128)} %copy.24), calls=%async_computation.2 | async-start | bytes 65536 | tf_op jit(solution)/shard_map/all_to_all | solution.py:71
  106.7 60.3 %all-to-all-start.1 = ((f32[128,64,128]{2,0,1:T(8,128)}), f32[128,64,128]{2,0,1:T(8,128)}, u32[]{:S(2)}, u32[]{:S(2)}) async-start(f32[128,64,128]{2,0,1:T(8,128)} %copy.27), calls=%async_computation.1 | async-start | bytes 8388608 | tf_op jit(solution)/shard_map/all_to_all | solution.py:40
  181.3 60.5 %all-to-all-start.3 = ((f32[128,64,128]{2,0,1:T(8,128)}), f32[128,64,128]{2,0,1:T(8,128)}, u32[]{:S(2)}, u32[]{:S(2)}) async-start(f32[128,64,128]{2,0,1:T(8,128)} %select_bitcast_fusion), calls=%async_computation.3 | async-start | bytes 8388608 | tf_op jit(solution)/shard_map/all_to_all | solution.py:74
  192.8 54.0 %copy-start.4 = (f32[8192]{0:T(1024)S(1)}, f32[8192]{0:T(1024)}, u32[]{:S(2)}) copy-start(f32[8192]{0:T(1024)} %param.13) | copy-start | bytes 98308
  336.9 6.1 %copy-start.11 = (u32[128]{0:T(128)S(1)}, u32[128]{0:T(128)}, u32[]{:S(2)}) copy-start(u32[128]{0:T(128)} %constant.78) | copy-start | bytes 1540
  336.9 7.4 %copy-start.7 = (f32[8192]{0:T(1024)S(1)}, f32[8192]{0:T(1024)}, u32[]{:S(2)}) copy-start(f32[8192]{0:T(1024)} %param.14) | copy-start | bytes 98308
  336.9 57.0 %all-to-all-start.5 = ((f32[128,64,128]{2,0,1:T(8,128)}), f32[128,64,128]{2,0,1:T(8,128)}, u32[]{:S(2)}, u32[]{:S(2)}) async-start(f32[128,64,128]{2,0,1:T(8,128)} %copy.31), calls=%async_computation.5 | async-start | bytes 8388608 | tf_op jit(solution)/shard_map/all_to_all | solution.py:40
  344.3 55.2 %copy-start.5 = (f32[8192]{0:T(1024)S(1)}, f32[8192]{0:T(1024)}, u32[]{:S(2)}) copy-start(f32[8192]{0:T(1024)} %param.15) | copy-start | bytes 98308
  399.5 18.8 %copy-start.6 = (f32[8192]{0:T(1024)S(1)}, f32[8192]{0:T(1024)}, u32[]{:S(2)}) copy-start(f32[8192]{0:T(1024)} %param.18) | copy-start | bytes 98308
  416.1 2.1 copy-start.2
  416.1 85.0 %copy-start.8 = (f32[128]{0:T(128)S(1)}, f32[128]{0:T(128)}, u32[]{:S(2)}) copy-start(f32[128]{0:T(128)} %param.19) | copy-start | bytes 1540
  416.1 103.2 %copy-start.1 = (bf16[64,128,128]{2,1,0:T(8,128)(2,1)S(1)}, bf16[64,128,128]{2,1,0:T(8,128)(2,1)}, u32[]{:S(2)}) copy-start(bf16[64,128,128]{2,1,0:T(8,128)(2,1)} %param.17) | copy-start | bytes 6291460
  501.1 18.2 %copy-start.9 = (f32[128]{0:T(128)}, f32[128]{0:T(128)S(1)}, u32[]{:S(2)}) copy-start(f32[128]{0:T(128)S(1)} %broadcast_multiply_fusion.3) | copy-start | bytes 1540
